TPU v7x, 128 devices: a whole 4x4x4 slice. The times are simulated.
128 devices in a mesh: lm: 8 (over z, x_hi), sl: 16 (over y, x_lo, core).
Axes of the slice: x: 4 (x_hi: 2, x_lo: 2; x = x_hi * 2 + x_lo), y: 4, z: 4, core: 2. Of those that a mesh axis runs over, the one named last changes fastest.
Arguments:
- slab: bfloat16 [16384, 1024], P('sl'), may hold values from -6 to 6
- landmarks: bfloat16 [32768, 1024], P(('lm', 'sl')), may hold values from -6 to 6
- codes: bfloat16 [32768, 96], P(('lm', 'sl')), may hold values from -4 to 4
- exponents: int32 [256], P(('lm', 'sl')), may hold values from -3 to 3
- eigvec: bfloat16 [96, 64], replicated, may hold values from -0.625 to 0.625
- ritz: float32 [64], replicated, may hold values from 0.5 to 4
Outputs:
- extended: float32 [16384, 64], P('sl')
All inputs are finite; a program needn't handle non-finite values.
Results may differ from a plain program's by a relative error of at most 0.004.
Values may be sent and summed in bfloat16 or wider, within the bound.
A program may use at most 128 MiB of HBM per device.

v0:
```python
import math
import jax
import jax.numpy as jnp
from jax import lax
from jax.sharding import PartitionSpec as P

BLOCK = 128


def local(slab, landmarks, codes, exponents, eigvec, ritz):
    total_land = codes.shape[0] * lax.axis_size("lm") * lax.axis_size("sl")
    coeff = 1.0 / math.sqrt(slab.shape[1])
    factor = 1.0 / (ritz * math.sqrt(total_land))
    scale = jnp.exp2(exponents.astype(jnp.float32))
    rows_scale = jnp.repeat(scale, BLOCK)
    basis = (codes.astype(jnp.float32) * rows_scale[:, None]).astype(jnp.bfloat16)
    vectors = jnp.dot(basis, eigvec, preferred_element_type=jnp.float32).astype(jnp.bfloat16)
    land = lax.all_gather(landmarks, "sl", axis=0, tiled=True)
    vec = lax.all_gather(vectors, "sl", axis=0, tiled=True)
    scores = jnp.dot(slab, land.T, preferred_element_type=jnp.float32) * coeff
    affinity = jnp.exp(scores).astype(jnp.bfloat16)
    terms = jnp.dot(affinity, vec, preferred_element_type=jnp.float32)
    summed = lax.psum(terms, "lm")
    return summed * factor[None, :]


def solution(mesh):
    return jax.shard_map(
        local,
        mesh=mesh,
        in_specs=(
            P("sl", None),
            P(("lm", "sl"), None),
            P(("lm", "sl"), None),
            P(("lm", "sl")),
            P(),
            P(),
        ),
        out_specs=P("sl", None),
        check_vma=False,
    )
```

profile of v0, /device:TPU:0, one launch (start us, length us, event | category | flops | bytes accessed | tf_op | source)
XLA Modules:
  0.0 178.2 jit_solution(8846013648305641239)
XLA Ops:
  6.5 0.0 copy-start
  6.5 0.0 all-gather.2.cloned.1.call-start
  6.5 0.7 all-gather.2.cloned.1.call-update
  7.3 0.0 all-reduce.2.cloned.1.call-start
  7.3 0.7 multiply_exponential_fusion
  8.0 0.1 broadcast_bitcast_fusion
  8.0 1.0 convolution_convert_fusion
  9.0 30.0 %all_gather.7 = bf16[4096,64]{1,0:T(8,128)(2,1)S(1)} all-gather(bf16[256,64]{1,0:T(8,128)(2,1)S(1)} %convolution_convert_fusion), channel_id=1, replica_groups=mesh['lm'=8,'sl'=16] {'sl'}, dimensions={0}, use_global_device_ids=true | all-gather | bytes 557056 | tf_op jit(solution)/shard_map/all_gather | solution.py:19
  39.1 0.0 copy-start.1
  39.1 27.3 %all-gather.2.cloned.1.call-done = bf16[4096,1024]{1,0:T(8,128)(2,1)} async-done(((bf16[256,1024]{1,0:T(8,128)(2,1)}), bf16[4096,1024]{1,0:T(8,128)(2,1)}) %all-gather.2.cloned.1.call-update) | async-done | bytes 8388624 | tf_op jit(solution)/shard_map/all_gather | solution.py:18
  66.4 0.0 copy-done
  66.4 15.6 %fusion.1 = f32[1024,64]{0,1:T(8,128)} fusion(bf16[4096,64]{1,0:T(8,128)(2,1)S(1)} %all_gather.7, bf16[1024,1024]{1,0:T(8,128)(2,1)S(1)} %copy-done, bf16[4096,1024]{1,0:T(8,128)(2,1)} %all-gather.2.cloned.1.call-done), kind=kOutput, calls=%fused_computation.8 | convolution fusion | flops 9135194112 | bytes 11272192 | tf_op jit(solution)/shard_map/dot_general | solution.py:22
  82.0 0.0 all-reduce.2.cloned.1.call-update
  82.0 0.0 copy-done.1
  82.0 87.6 %all-reduce.2.cloned.1.call-done = f32[1024,64]{0,1:T(8,128)} async-done(((f32[1024,64]{0,1:T(8,128)}), f32[1024,64]{0,1:T(8,128)}) %all-reduce.2.cloned.1.call-update) | async-done | bytes 262160 | tf_op jit(solution)/shard_map/psum | solution.py:23
  169.6 1.7 broadcast_multiply_fusion
  (1 shorter events, 0.0 us)
Async XLA Ops:
  6.5 59.8 %copy-start = (bf16[1024,1024]{1,0:T(8,128)(2,1)S(1)}, bf16[1024,1024]{1,0:T(8,128)(2,1)}, u32[]{:S(2)}) copy-start(bf16[1024,1024]{1,0:T(8,128)(2,1)} %param.6) | copy-start | bytes 6291460
  6.5 59.8 %all-gather.2.cloned.1.call-start = ((), (), s32[]{:S(2)}) async-start(), calls=%async_computation | async-start | bytes 8912896 | tf_op jit(solution)/shard_map/all_gather | solution.py:18
  7.3 162.3 %all-reduce.2.cloned.1.call-start = ((), (), s32[]{:S(2)}) async-start(), calls=%async_computation.1 | async-start | bytes 524288 | tf_op jit(solution)/shard_map/psum | solution.py:23
  39.1 42.9 %copy-start.1 = (f32[64]{0:T(128)S(1)}, f32[64]{0:T(128)}, u32[]{:S(2)}) copy-start(f32[64]{0:T(128)} %param.11) | copy-start | bytes 772
Sparse Core Ops, SparseCore 0:
  9.1 57.2 all-gather.1
  82.1 87.4 all-reduce.1
where the time goes:
time: 178 us
  waiting for transfers between devices  116 us (65%)
  blocking collectives  30 us (17%)
  matrix products  16.6 us (9%)
  between operations  13.4 us (8%)
  other arithmetic  2.4 us (1%)
    psum x1, waiting for transfers between devices, local(): summed = lax.psum(terms, 'lm')  87.6 us
    all_gather x1, blocking collectives, local(): vec = lax.all_gather(vectors, 'sl', axis=0, tiled=True)  30 us
    all_gather x1, waiting for transfers between devices, local(): land = lax.all_gather(landmarks, 'sl', axis=0, tiled=True)  27.3 us
    dot_general x1, matrix products, local(): terms = jnp.dot(affinity, vec, preferred_element_type=jnp.float32)  15.6 us
  transfers between devices with their start and end apart: 2, of which 2 were waited for; matrix products, arithmetic and copies ran while one was open for 1% of the time, Pallas kernels for 0%

commit v1 on v0

--- a/solution.py
+++ b/solution.py
@@ -15,7 +15,9 @@
     rows_scale = jnp.repeat(scale, BLOCK)
     basis = (codes.astype(jnp.float32) * rows_scale[:, None]).astype(jnp.bfloat16)
     vectors = jnp.dot(basis, eigvec, preferred_element_type=jnp.float32).astype(jnp.bfloat16)
-    land = lax.all_gather(landmarks, "sl", axis=0, tiled=True)
+    land = jnp.concatenate(
+        lax.all_to_all(jnp.stack([landmarks] * lax.axis_size("sl")), "sl", 0, 0), axis=0
+    )
     vec = lax.all_gather(vectors, "sl", axis=0, tiled=True)
     scores = jnp.dot(slab, land.T, preferred_element_type=jnp.float32) * coeff
     affinity = jnp.exp(scores).astype(jnp.bfloat16)

time: 178 us -> 240 us (1.35)
  blocking collectives: 30 us -> 113 us
  waiting for transfers between devices: 116 us -> 84.3 us
  starting transfers between devices: 0.04 us -> 5.81 us
  local copies, waits for them, and re-layouts: 0.08 us -> 5.58 us
    all_gather x1, blocking collectives: 30 us -> 113 us  [local(): vec = lax.all_gather(vectors, 'sl', axis=0, tiled=True)]
    all_gather x1 -> x0, waiting for transfers between devices: 27.3 us -> none  [local(): land = lax.all_gather(landmarks, 'sl', axis=0, tiled=True)]
    all_to_all x0 -> x1, starting transfers between devices: none -> 5.77 us  [local(): lax.all_to_all(jnp.stack([landmarks] * lax.axis_size('sl')), 'sl', 0, 0)]
    another operation x0 -> x1, local copies, waits for them, and re-layouts: none -> 5.49 us  [local(): jnp.stack([landmarks] * lax.axis_size('sl'))]
    psum x1, waiting for transfers between devices: 87.6 us -> 84.3 us  [local(): summed = lax.psum(terms, 'lm')]
  transfers between devices with their start and end apart: 2 -> 2, of which waited for: 2 -> 1; matrix products, arithmetic and copies ran while one was open for 1% -> 0% of each run, Pallas kernels for 0% -> 0%
where the time goes in v1:
time: 240 us; the launch traced here: 239 us
  blocking collectives  113 us (47%)
  waiting for transfers between devices  84.3 us (35%)
  matrix products  15.8 us (7%)
  between operations  13.4 us (6%)
  starting transfers between devices  5.81 us (2%)
  local copies, waits for them, and re-layouts  5.58 us (2%)
    all_gather x1, blocking collectives, local(): vec = lax.all_gather(vectors, 'sl', axis=0, tiled=True)  113 us
    psum x1, waiting for transfers between devices, local(): summed = lax.psum(terms, 'lm')  84.3 us
    dot_general x1, matrix products, local(): terms = jnp.dot(affinity, vec, preferred_element_type=jnp.float32)  15.6 us
    all_to_all x1, starting transfers between devices, local(): lax.all_to_all(jnp.stack([landmarks] * lax.axis_size('sl')), 'sl', 0, 0)  5.77 us
    another operation x1, local copies, waits for them, and re-layouts, local(): jnp.stack([landmarks] * lax.axis_size('sl'))  5.49 us
  transfers between devices with their start and end apart: 2, of which 1 were waited for; matrix products, arithmetic and copies ran while one was open for 0% of the time, Pallas kernels for 0%

profile of v1, /device:TPU:0, one launch (start us, length us, event | category | flops | bytes accessed | tf_op | source)
XLA Modules:
  0.0 239.4 jit_solution(3695207675596308)
XLA Ops:
  6.5 0.0 copy-start
  6.5 5.5 %stack.2 = bf16[16,256,1024]{2,1,0:T(8,128)(2,1)} broadcast(bf16[256,1024]{1,0:T(8,128)(2,1)} %param.7), dimensions={1,2} | broadcast | bytes 8912896 | tf_op jit(solution)/shard_map/stack | solution.py:19
  12.0 0.0 copy-start.3
  12.0 0.0 copy-start.1
  12.0 0.0 copy-start.2
  12.0 5.8 %all-to-all-start = ((bf16[16,256,1024]{2,1,0:T(8,128)(2,1)}), bf16[16,256,1024]{2,1,0:T(8,128)(2,1)}, u32[]{:S(2)}, u32[]{:S(2)}) async-start(bf16[16,256,1024]{2,1,0:T(8,128)(2,1)} %stack.2), calls=%async_computation | async-start | bytes 16777216 | tf_op jit(solution)/shard_map/all_to_all | solution.py:19
  17.8 0.0 all-reduce.2.cloned.1.call-start
  17.9 0.0 copy-done.3
  17.9 0.1 broadcast_bitcast_fusion
  18.0 0.0 copy-done.1
  18.0 0.0 copy-done.2
  18.0 0.2 convolution_convert_fusion
  18.2 112.7 %all_gather.3 = bf16[4096,64]{1,0:T(8,128)(2,1)S(1)} all-gather(bf16[256,64]{1,0:T(8,128)(2,1)S(1)} %convolution_convert_fusion), channel_id=1, replica_groups=mesh['lm'=8,'sl'=16] {'sl'}, dimensions={0}, use_global_device_ids=true | all-gather | bytes 557056 | tf_op jit(solution)/shard_map/all_gather | solution.py:21
  130.8 0.0 all-to-all-done
  130.9 0.0 copy-done
  130.9 0.0 copy-start.4
  130.9 15.6 %fusion.1 = f32[1024,64]{0,1:T(8,128)} fusion(bf16[4096,64]{1,0:T(8,128)(2,1)S(1)} %all_gather.3, bf16[1024,1024]{1,0:T(8,128)(2,1)S(1)} %copy-done, bf16[4096,1024]{1,0:T(8,128)(2,1)} %bitcast), kind=kOutput, calls=%fused_computation.8 | convolution fusion | flops 9135194112 | bytes 11272192 | tf_op jit(solution)/shard_map/dot_general | solution.py:24
  146.5 0.0 all-reduce.2.cloned.1.call-update
  146.5 0.0 copy-done.4
  146.5 84.3 %all-reduce.2.cloned.1.call-done = f32[1024,64]{0,1:T(8,128)} async-done(((f32[1024,64]{0,1:T(8,128)}), f32[1024,64]{0,1:T(8,128)}) %all-reduce.2.cloned.1.call-update) | async-done | bytes 262160 | tf_op jit(solution)/shard_map/psum | solution.py:25
  230.8 1.7 broadcast_multiply_fusion
  (2 shorter events, 0.0 us)
Async XLA Ops:
  6.5 124.3 %copy-start = (bf16[1024,1024]{1,0:T(8,128)(2,1)S(1)}, bf16[1024,1024]{1,0:T(8,128)(2,1)}, u32[]{:S(2)}) copy-start(bf16[1024,1024]{1,0:T(8,128)(2,1)} %param.6) | copy-start | bytes 6291460
  12.0 5.8 %copy-start.3 = (s32[2]{0:T(128)S(1)}, s32[2]{0:T(128)}, u32[]{:S(2)}) copy-start(s32[2]{0:T(128)} %param.9) | copy-start | bytes 28
  12.0 5.9 %copy-start.1 = (bf16[256,96]{0,1:T(8,128)(2,1)S(1)}, bf16[256,96]{0,1:T(8,128)(2,1)}, u32[]{:S(2)}) copy-start(bf16[256,96]{0,1:T(8,128)(2,1)} %param.8) | copy-start | bytes 147460
  12.0 5.9 %copy-start.2 = (bf16[96,64]{0,1:T(8,128)(2,1)S(1)}, bf16[96,64]{0,1:T(8,128)(2,1)}, u32[]{:S(2)}) copy-start(bf16[96,64]{0,1:T(8,128)(2,1)} %param.10) | copy-start | bytes 36868
  12.0 118.8 %all-to-all-start = ((bf16[16,256,1024]{2,1,0:T(8,128)(2,1)}), bf16[16,256,1024]{2,1,0:T(8,128)(2,1)}, u32[]{:S(2)}, u32[]{:S(2)}) async-start(bf16[16,256,1024]{2,1,0:T(8,128)(2,1)} %stack.2), calls=%async_computation | async-start | bytes 16777216 | tf_op jit(solution)/shard_map/all_to_all | solution.py:19
  17.8 213.0 %all-reduce.2.cloned.1.call-start = ((), (), s32[]{:S(2)}) async-start(), calls=%async_computation.1 | async-start | bytes 524288 | tf_op jit(solution)/shard_map/psum | solution.py:25
  130.9 15.6 %copy-start.4 = (f32[64]{0:T(128)S(1)}, f32[64]{0:T(128)}, u32[]{:S(2)}) copy-start(f32[64]{0:T(128)} %param.11) | copy-start | bytes 772
Sparse Core Ops, SparseCore 0:
  146.6 84.1 all-reduce.1
